TPU v7x, 32 devices: a whole 2x2x4 slice. The times are simulated.
32 devices in a mesh: ada: 4 (over y, core), avg: 8 (over z, x).
Axes of the slice: x: 2, y: 2, z: 4, core: 2. Of those that a mesh axis runs over, the one named last changes fastest.
Arguments:
- edges: float32 [49152, 1536], P(('ada', 'avg')), may hold values from -6 to 6
- teacher: float32 [49152, 512], P(('ada', 'avg')), may hold values from -9.5 to 9.5
- w_first: float32 [1536, 512], replicated, may hold values from -0.15625 to 0.15625
- b_first: float32 [512], replicated, may hold values from -3 to 3
- w_second: float32 [512, 512], replicated, may hold values from -0.25 to 0.25
- b_second: float32 [512], replicated, may hold values from -3 to 3
- norm_gain: float32 [512], replicated, may hold values from 0.5 to 1.5
- norm_shift: float32 [512], replicated, may hold values from -3 to 3
Outputs:
- new_w_first: float32 [1536, 512], replicated
- new_b_first: float32 [512], replicated
- new_w_second: float32 [512, 512], replicated
- new_b_second: float32 [512], replicated
- new_gain: float32 [512], replicated
- new_shift: float32 [512], replicated
All inputs are finite; a program needn't handle non-finite values.
Results may differ from a plain program's by a relative error of at most 0.0003.
Values sent between devices are 32-bit elements; how exact they have to be, the bound alone decides.
A program may use at most 128 MiB of HBM per device.

v0:
```python
import jax
import jax.numpy as jnp
from jax import lax
from jax.sharding import PartitionSpec as P

norm_eps = 1e-06
step_rate = 2.0
high = lax.Precision.HIGHEST


def swapped(block, axis, bit):
    count = lax.axis_size(axis)
    route = []
    for low in range(count):
        high = low | 1 << bit
        if high != low and high < count:
            route += [(low, high), (high, low)]
    return lax.ppermute(block, axis, route)


def local_loss(params, inputs, targets):
    w_first, b_first, w_second, b_second, norm_gain, norm_shift = params
    zfirst = jnp.dot(inputs, w_first, precision=high, preferred_element_type=jnp.float32) + b_first
    hidden = zfirst * jax.nn.sigmoid(zfirst)
    zsecond = (
        jnp.dot(hidden, w_second, precision=high, preferred_element_type=jnp.float32) + b_second
    )
    center = zsecond - jnp.mean(zsecond, axis=1, keepdims=True)
    spread = jnp.mean(center * center, axis=1, keepdims=True)
    output = center * lax.rsqrt(spread + 1e-05) * norm_gain + norm_shift
    return 0.5 * jnp.sum((output - targets) ** 2) / inputs.shape[0]


def split_half(array, axis_dim, upper_side):
    half = array.shape[axis_dim] // 2
    lower_half = lax.slice_in_dim(array, 0, half, axis=axis_dim)
    upper_half = lax.slice_in_dim(array, half, 2 * half, axis=axis_dim)
    keep = jnp.where(upper_side, upper_half, lower_half)
    send = jnp.where(upper_side, lower_half, upper_half)
    return (keep, send)


def level_stats(kept, got, upper_side):
    first = jnp.stack(
        [jnp.sum(kept[0] * got[0]), jnp.sum(kept[0] * kept[0]), jnp.sum(got[0] * got[0])]
    )
    second = jnp.stack(
        [jnp.sum(kept[1] * got[1]), jnp.sum(kept[1] * kept[1]), jnp.sum(got[1] * got[1])]
    )
    vectors = jnp.stack(
        [
            jnp.sum(kept[2] * got[2], axis=1),
            jnp.sum(kept[2] * kept[2], axis=1),
            jnp.sum(got[2] * got[2], axis=1),
        ]
    )
    stats = jnp.concatenate([first[:, None], second[:, None], vectors], axis=1)
    lower_norm = jnp.where(upper_side, stats[2], stats[1])
    upper_norm = jnp.where(upper_side, stats[1], stats[2])
    return jnp.stack([stats[0], lower_norm, upper_norm])


def local(edges, teacher, w_first, b_first, w_second, b_second, norm_gain, norm_shift):
    params = (w_first, b_first, w_second, b_second, norm_gain, norm_shift)
    grads = jax.grad(local_loss)(params, edges, teacher)
    vector_grad = jnp.stack([grads[1], grads[3], grads[4], grads[5]])
    pieces = (grads[0], grads[2], vector_grad)
    split_dims = (0, 0, 1)
    ada_count = lax.axis_size("ada")
    avg_count = lax.axis_size("avg")
    levels = ada_count.bit_length() - 1
    rank_ada = lax.axis_index("ada")
    for level in range(levels):
        bit = levels - 1 - level
        upper_side = rank_ada // 2**bit % 2 == 1
        kept = []
        sending = []
        for array, axis_dim in zip(pieces, split_dims):
            keep, send = split_half(array, axis_dim, upper_side)
            kept.append(keep)
            sending.append(send)
        got = swapped((sending[0], sending[1], sending[2]), "ada", bit)
        stats = level_stats(kept, got, upper_side)
        totals = stats
        for level_bit in range(bit, levels):
            totals = totals + swapped(totals, "ada", level_bit)
        own_norm = jnp.where(upper_side, totals[2], totals[1])
        other_norm = jnp.where(upper_side, totals[1], totals[2])
        coef_mine = 1.0 - totals[0] / (2.0 * (own_norm + norm_eps))
        coef_other = 1.0 - totals[0] / (2.0 * (other_norm + norm_eps))
        pieces = (
            coef_mine[0] * kept[0] + coef_other[0] * got[0],
            coef_mine[1] * kept[1] + coef_other[1] * got[1],
            coef_mine[2:, None] * kept[2] + coef_other[2:, None] * got[2],
        )
    vector_params = jnp.stack([b_first, b_second, norm_gain, norm_shift])
    full_params = (w_first, w_second, vector_params)
    sums = lax.psum((pieces[0], pieces[1], pieces[2]), "avg")
    updated = []
    for total, whole, axis_dim in zip(sums, full_params, split_dims):
        count = total.shape[axis_dim]
        mine = lax.dynamic_slice_in_dim(whole, rank_ada * count, count, axis_dim)
        updated.append(mine - step_rate * (total / avg_count))
    result = (
        lax.all_gather(updated[0], "ada", axis=0, tiled=True),
        lax.all_gather(updated[1], "ada", axis=0, tiled=True),
        lax.all_gather(updated[2], "ada", axis=1, tiled=True),
    )
    new_first, new_second, new_vectors = result
    return (new_first, new_vectors[0], new_second, new_vectors[1], new_vectors[2], new_vectors[3])


def solution(mesh):
    in_specs = (P(("ada", "avg"), None), P(("ada", "avg"), None), P(), P(), P(), P(), P(), P())
    out_specs = (P(), P(), P(), P(), P(), P())
    return jax.shard_map(local, mesh=mesh, in_specs=in_specs, out_specs=out_specs, check_vma=False)
```

profile of v0, /device:TPU:0, one launch (start us, length us, event | category | flops | bytes accessed | tf_op | source)
XLA Modules:
  0.0 310.2 jit_solution(3395414795068266566)
XLA Ops:
  8.1 3.6 %copy.22 = f32[1536,512]{0,1:T(8,128)} copy(f32[1536,512]{1,0:T(8,128)} %param.9) | data formatting | bytes 6291456 | tf_op args[1]
  11.7 17.7 %convolution_add_fusion.1 = f32[1536,512]{1,0:T(8,128)S(1)} fusion(f32[1536,1536]{1,0:T(8,128)} %param.8, f32[1536,512]{1,0:T(8,128)S(1)} %copy-done, f32[512]{0:T(512)S(1)} %copy-done.9), kind=kOutput, calls=%fused_computation.4 | convolution fusion | flops 14496301056 | bytes 15730688 | tf_op jit(solution)/shard_map/jvp()/dot_general | solution.py:23
  29.4 6.1 %fusion.46 = (f32[1536]{0:T(1024)S(1)}, f32[1536,512]{0,1:T(8,128)S(1)}) fusion(f32[512]{0:T(512)S(1)} %copy-done.10, f32[512,512]{1,0:T(8,128)S(1)} %copy-done.6, f32[1536,512]{1,0:T(8,128)S(1)} %convolution_add_fusion.1), kind=kOutput, calls=%fused_computation.123 | convolution fusion | flops 4836555264 | bytes 7348224 | tf_op jit(solution)/shard_map/jvp()/dot_general | solution.py:26
  37.5 2.4 multiply_reduce_fusion
  41.5 11.2 %fusion.47 = (f32[512]{0:T(512)S(1)}, f32[1536,512]{1,0:T(8,128)S(1)}) fusion(f32[1536,512]{1,0:T(8,128)S(1)} %convolution_add_fusion.1, f32[512,512]{1,0:T(8,128)S(1)} %copy-done.6, f32[1536,512]{0,1:T(8,128)S(1)} %get-tuple-element.48, f32[1536]{0:T(1024)S(1)} %negate_multiply_fusion), kind=kOutput, calls=%fused_computation.124 | convolution fusion | flops 4840488448 | bytes 10493952 | tf_op jit(solution)/shard_map/transpose(jvp())/dot_general | solution.py:26
  52.8 16.5 %convolution_bitcast_fusion = f32[1536,512]{0,1:T(8,128)S(1)} fusion(f32[1536,512]{1,0:T(8,128)S(1)} %get-tuple-element.74, f32[1536,1536]{1,0:T(8,128)S(1)} %bitcast.81), kind=kOutput, calls=%fused_computation.3 | convolution fusion | flops 14495514624 | bytes 15728640 | tf_op jit(solution)/shard_map/transpose(jvp())/dot_general | solution.py:23
  70.8 3.0 collective-permute-start
  73.8 10.6 %fusion.3 = f32[512,512]{1,0:T(8,128)S(1)} fusion(f32[1536,512]{0,1:T(8,128)S(1)} %get-tuple-element.48, f32[1536]{0:T(1024)S(1)} %negate_multiply_fusion, f32[1536,512]{1,0:T(8,128)S(1)} %convolution_add_fusion.1), kind=kOutput, calls=%fused_computation.15 | convolution fusion | flops 4835770368 | bytes 7346176 | tf_op jit(solution)/shard_map/transpose(jvp())/dot_general | solution.py:26
  87.8 32.0 %collective-permute-done.2 = f32[4,256]{1,0:T(4,128)S(1)} collective-permute-done((f32[4,256]{1,0:T(4,128)S(1)}, f32[4,256]{1,0:T(4,128)S(1)}, u32[]{:S(2)}, u32[]{:S(2)}) %collective-permute-start.2) | collective-permute-done | bytes 4128 | tf_op jit(solution)/shard_map/ppermute | solution.py:18
  120.0 2.9 multiply_reduce_fusion.12
  125.0 4.4 %multiply_reduce_fusion.6 = (f32[]{:T(128)}, f32[]{:T(128)}, f32[]{:T(128)}, f32[768,512]{0,1:T(8,128)}) fusion(f32[768,512]{0,1:T(8,128)} %collective-permute-done, f32[1536,512]{0,1:T(8,128)} %copy-done.3, pred[]{:T(512)S(6)} %eq.10), kind=kLoop, calls=%fused_computation.22 | loop fusion | flops 2752509 | bytes 6291469 | tf_op jit(solution)/shard_map/reduce_sum | solution.py:45
  136.0 2.6 multiply_add_fusion.2
  138.7 2.9 multiply_add_fusion
  150.2 3.3 %multiply_reduce_fusion.9 = (f32[]{:T(128)}, f32[]{:T(128)}, f32[]{:T(128)}, f32[384,512]{0,1:T(8,128)}) fusion(f32[384,512]{0,1:T(8,128)} %collective-permute-done.4, f32[768,512]{0,1:T(8,128)} %copy-done.2, pred[]{:T(512)S(6)} %eq.9), kind=kLoop, calls=%fused_computation.31 | loop fusion | flops 1376253 | bytes 3145741 | tf_op jit(solution)/shard_map/reduce_sum | solution.py:45
  161.8 3.6 %multiply_add_fusion.1 = f32[384,512]{0,1:T(8,128)} fusion(f32[384,512]{0,1:T(8,128)} %collective-permute-done.4, f32[384,512]{0,1:T(8,128)} %get-tuple-element.41, f32[]{:T(128)} %bitcast.34, f32[]{:T(128)} %bitcast.33), kind=kLoop, calls=%fused_computation.28 | loop fusion | flops 589824 | bytes 2359304 | tf_op jit(solution)/shard_map/add | solution.py:92
  165.4 3.0 multiply_add_fusion.3
  168.4 79.9 %all-reduce.3.cloned.1.call-done = (f32[384,512]{0,1:T(8,128)}, f32[128,512]{1,0:T(8,128)}) async-done(((f32[384,512]{0,1:T(8,128)}, f32[128,512]{1,0:T(8,128)}), (f32[384,512]{0,1:T(8,128)}, f32[128,512]{1,0:T(8,128)})) %all-reduce.3.cloned.1.call-update) | async-done | bytes 1048592 | tf_op jit(solution)/shard_map/psum | solution.py:98
  251.2 2.3 copy.28
  253.4 2.3 multiply_subtract_fusion
  256.0 20.1 %psum.22 = f32[4,128]{1,0:T(4,128)S(1)} all-reduce(f32[4,128]{1,0:T(4,128)S(1)} %multiply_add_fusion.6), channel_id=1, replica_groups=mesh['ada'=4,'avg'=8] {'avg'}, use_global_device_ids=true, to_apply=%region_27.28 | all-reduce | flops 512 | bytes 4096 | tf_op jit(solution)/shard_map/psum | solution.py:98
  276.2 5.2 %all_gather.10 = f32[4,512]{1,0:T(4,128)S(1)} all-gather(f32[4,128]{1,0:T(4,128)S(1)} %fusion.17), channel_id=1, replica_groups=mesh['ada'=4,'avg'=8] {'ada'}, dimensions={1}, use_global_device_ids=true | all-gather | bytes 10240 | tf_op jit(solution)/shard_map/all_gather | solution.py:107
  282.0 15.4 %all-gather.3.cloned.1.call-done = f32[1536,512]{0,1:T(8,128)} async-done(((f32[384,512]{0,1:T(8,128)}), f32[1536,512]{0,1:T(8,128)}) %all-gather.3.cloned.1.call-update) | async-done | bytes 3145744 | tf_op jit(solution)/shard_map/all_gather | solution.py:105
  297.5 3.5 %copy.27 = f32[1536,512]{1,0:T(8,128)} copy(f32[1536,512]{0,1:T(8,128)} %all-gather.3.cloned.1.call-done) | data formatting | bytes 6291456
  301.0 2.3 copy.32
  (101 shorter events, 38.7 us)
Async XLA Ops:
  7.2 4.5 %copy-start = (f32[1536,512]{1,0:T(8,128)S(1)}, f32[1536,512]{1,0:T(8,128)}, u32[]{:S(2)}) copy-start(f32[1536,512]{1,0:T(8,128)} %param.10) | copy-start | bytes 9437188
  7.2 241.2 %all-reduce.3.cloned.1.call-start = ((), (), s32[]{:S(2)}) async-start(), calls=%async_computation.2 | async-start | bytes 2097152 | tf_op jit(solution)/shard_map/psum | solution.py:98
  8.1 3.6 %copy-start.9 = (f32[512]{0:T(512)S(1)}, f32[512]{0:T(512)}, u32[]{:S(2)}) copy-start(f32[512]{0:T(512)} %param.11) | copy-start | bytes 6148
  11.7 17.7 %copy-start.6 = (f32[512,512]{1,0:T(8,128)S(1)}, f32[512,512]{1,0:T(8,128)}, u32[]{:S(2)}) copy-start(f32[512,512]{1,0:T(8,128)} %param.12) | copy-start | bytes 3145732
  11.7 17.7 %copy-start.10 = (f32[512]{0:T(512)S(1)}, f32[512]{0:T(512)}, u32[]{:S(2)}) copy-start(f32[512]{0:T(512)} %param.13) | copy-start | bytes 6148
  35.6 1.9 copy-start.1
  35.6 1.9 copy-start.7
  35.6 1.9 copy-start.8
  39.9 12.8 %slice-start = ((s8[9437184]{0:T(1024)(128)(4,1)}), s8[1048576]{0:T(1024)(128)(4,1)S(1)}, s32[]{:S(2)}) async-start(s8[9437184]{0:T(1024)(128)(4,1)} %bitcast.80), calls=%async_computation.3 | async-start | bytes 2097152
  41.5 11.2 %slice-start.1 = ((s8[9437184]{0:T(1024)(128)(4,1)}), s8[4194304]{0:T(1024)(128)(4,1)S(1)}, s32[]{:S(2)}) async-start(s8[9437184]{0:T(1024)(128)(4,1)} %bitcast.80), calls=%async_computation.4 | async-start | bytes 8388608
  41.5 11.2 %slice-start.2 = ((s8[9437184]{0:T(1024)(128)(4,1)}), s8[4194304]{0:T(1024)(128)(4,1)S(1)}, s32[]{:S(2)}) async-start(s8[9437184]{0:T(1024)(128)(4,1)} %bitcast.80), calls=%async_computation.5 | async-start | bytes 8388608
  69.3 15.1 %copy-start.3 = (f32[1536,512]{0,1:T(8,128)}, f32[1536,512]{0,1:T(8,128)S(1)}, u32[]{:S(2)}) copy-start(f32[1536,512]{0,1:T(8,128)S(1)} %convolution_bitcast_fusion) | copy-start | bytes 9437188
  70.8 54.2 %collective-permute-start = (f32[768,512]{0,1:T(8,128)}, f32[768,512]{0,1:T(8,128)}, u32[]{:S(2)}, u32[]{:S(2)}) collective-permute-start(f32[768,512]{0,1:T(8,128)} %slice_select_fusion), channel_id=1, source_target_pairs={{0,16},{16,0},{8,24},{24,8},{1,17},{17,1},{9,25},{25,9},{2,18},{18... | collective-permute-start | bytes 4718600 | tf_op jit(solution)/shard_map/ppermute | solution.py:18
  85.4 34.5 %collective-permute-start.1 = (f32[256,512]{1,0:T(8,128)}, f32[256,512]{1,0:T(8,128)}, u32[]{:S(2)}, u32[]{:S(2)}) collective-permute-start(f32[256,512]{1,0:T(8,128)} %slice_select_fusion.4), channel_id=1, source_target_pairs={{0,16},{16,0},{8,24},{24,8},{1,17},{17,1},{9,25},{25,9},{2,18},{18... | collective-permute-start | bytes 1572872 | tf_op jit(solution)/shard_map/ppermute | solution.py:18
  85.8 34.1 %collective-permute-start.2 = (f32[4,256]{1,0:T(4,128)S(1)}, f32[4,256]{1,0:T(4,128)S(1)}, u32[]{:S(2)}, u32[]{:S(2)}) collective-permute-start(f32[4,256]{1,0:T(4,128)S(1)} %slice_select_fusion.8), channel_id=1, source_target_pairs={{0,16},{16,0},{8,24},{24,8},{1,17},{17,1},{9,25},{25,9},{2,18},{18... | collective-permute-start | bytes 12296 | tf_op jit(solution)/shard_map/ppermute | solution.py:18
  131.7 3.7 %collective-permute-start.3 = (f32[3,6]{1,0:T(4,128)S(1)}, f32[3,6]{1,0:T(4,128)S(1)}, u32[]{:S(2)}, u32[]{:S(2)}) collective-permute-start(f32[3,6]{1,0:T(4,128)S(1)} %pad_maximum_fusion.1), channel_id=1, source_target_pairs={{0,16},{16,0},{8,24},{24,8},{1,17},{17,1},{9,25},{25,9},{2,18},{18... | collective-permute-start | bytes 224 | tf_op jit(solution)/shard_map/ppermute | solution.py:18
  133.5 5.3 %copy-start.4 = (f32[768,512]{0,1:T(8,128)S(1)}, f32[768,512]{0,1:T(8,128)}, u32[]{:S(2)}) copy-start(f32[768,512]{0,1:T(8,128)} %get-tuple-element.44) | copy-start | bytes 4718596
  138.7 8.0 %collective-permute-start.5 = (f32[128,512]{1,0:T(8,128)S(1)}, f32[128,512]{1,0:T(8,128)S(1)}, u32[]{:S(2)}, u32[]{:S(2)}) collective-permute-start(f32[128,512]{1,0:T(8,128)S(1)} %slice_select_fusion.6), channel_id=1, source_target_pairs={{0,8},{8,0},{16,24},{24,16},{1,9},{9,1},{17,25},{25,17},{2,10},{10... | collective-permute-start | bytes 786440 | tf_op jit(solution)/shard_map/ppermute | solution.py:18
  143.8 6.4 %collective-permute-start.4 = (f32[384,512]{0,1:T(8,128)}, f32[384,512]{0,1:T(8,128)}, u32[]{:S(2)}, u32[]{:S(2)}) collective-permute-start(f32[384,512]{0,1:T(8,128)} %slice_select_fusion.2), channel_id=1, source_target_pairs={{0,8},{8,0},{16,24},{24,16},{1,9},{9,1},{17,25},{25,17},{2,10},{10... | collective-permute-start | bytes 2359304 | tf_op jit(solution)/shard_map/ppermute | solution.py:18
  144.3 2.2 collective-permute-start.6
  155.6 1.3 collective-permute-start.7
  156.9 3.7 %collective-permute-start.8 = (f32[3,6]{1,0:T(4,128)S(1)}, f32[3,6]{1,0:T(4,128)S(1)}, u32[]{:S(2)}, u32[]{:S(2)}) collective-permute-start(f32[3,6]{1,0:T(4,128)S(1)} %fusion.36), channel_id=1, source_target_pairs={{0,16},{16,0},{8,24},{24,8},{1,17},{17,1},{9,25},{25,9},{2,18},{18... | collective-permute-start | bytes 224 | tf_op jit(solution)/shard_map/ppermute | solution.py:18
  168.4 113.7 %all-gather.5.cloned.1.call-start = ((), (), s32[]{:S(2)}) async-start(), calls=%async_computation.1 | async-start | bytes 1310720 | tf_op jit(solution)/shard_map/all_gather | solution.py:106
  250.2 47.3 %all-gather.3.cloned.1.call-start = ((), (), s32[]{:S(2)}) async-start(), calls=%async_computation | async-start | bytes 3932160 | tf_op jit(solution)/shard_map/all_gather | solution.py:105
  (2 other events, 2.4 us)
Sparse Core Ops, SparseCore 0:
  168.5 79.8 all-reduce.2
  250.3 16.3 all-gather.4
  268.9 28.5 all-gather.2
where the time goes:
time: 316 us; the launch traced here: 310 us
  waiting for transfers between devices  134 us (42%)
  matrix products  62.2 us (20%)
  other arithmetic  46.1 us (15%)
  blocking collectives  25.4 us (8%)
  local copies, waits for them, and re-layouts  18.2 us (6%)
  between operations  14.5 us (5%)
  starting transfers between devices  9.85 us (3%)
    psum x1, waiting for transfers between devices, local(): sums = lax.psum((pieces[0], pieces[1], pieces[2]), 'avg')  79.9 us
    ppermute x9, waiting for transfers between devices, swapped(): return lax.ppermute(block, axis, route)  38.6 us
    dot_general x2, matrix products, local_loss(): jnp.dot(inputs, w_first, precision=high, preferred_element_type=jnp.float32)  34.2 us
    dot_general x3, matrix products, local_loss(): jnp.dot(hidden, w_second, precision=high, preferred_element_type=jnp.floa...  27.9 us
    psum x1, blocking collectives, local(): sums = lax.psum((pieces[0], pieces[1], pieces[2]), 'avg')  20.1 us
    all_gather x1, waiting for transfers between devices, local(): lax.all_gather(updated[0], 'ada', axis=0, tiled=True)  15.4 us
    unnamed x32, local copies, waits for them, and re-layouts  14.3 us
    ppermute x9, starting transfers between devices, swapped(): return lax.ppermute(block, axis, route)  9.73 us
  transfers between devices with their start and end apart: 12, of which 7 were waited for; matrix products, arithmetic and copies ran while one was open for 10% of the time, Pallas kernels for 0%

commit v1 on v0

v1 whole, which is shorter than its diff:
```python
import functools

import jax
import jax.numpy as jnp
from jax import lax
from jax.experimental import pallas as pl
from jax.experimental.pallas import tpu as pltpu
from jax.sharding import PartitionSpec as P

norm_eps = 1e-06
step_rate = 2.0
prec = lax.Precision.HIGH


def local_loss(params, inputs, targets):
    w_first, b_first, w_second, b_second, norm_gain, norm_shift = params
    zfirst = jnp.dot(inputs, w_first, precision=prec, preferred_element_type=jnp.float32) + b_first
    hidden = zfirst * jax.nn.sigmoid(zfirst)
    zsecond = (
        jnp.dot(hidden, w_second, precision=prec, preferred_element_type=jnp.float32) + b_second
    )
    center = zsecond - jnp.mean(zsecond, axis=1, keepdims=True)
    spread = jnp.mean(center * center, axis=1, keepdims=True)
    output = center * lax.rsqrt(spread + 1e-05) * norm_gain + norm_shift
    return 0.5 * jnp.sum((output - targets) ** 2) / inputs.shape[0]


class Sizes:
    def __init__(self, n_ada, n_avg, width):
        self.n_ada, self.n_avg, self.width = n_ada, n_avg, width
        self.core = 2 if n_ada % 2 == 0 else 1
        self.y = n_ada // self.core
        self.x = self.y if n_avg % self.y == 0 else 1
        self.z = n_avg // self.x
        self.cols = width // self.x
        self.levels = n_ada.bit_length() - 1
        self.stat_rows = -(-3 * (n_ada // 2) // 8) * 8

    def tensor_copies(self):
        gather = 2 * (self.z - 1) + self.x - 1 + 2 * (self.y - 1) + self.y * (self.x - 1)
        gather += 2 * self.y * (self.core - 1)
        scatter = 2 * (self.x - 1) + 2 * (self.z - 1)
        return (1 + self.levels) * (self.n_ada - 1) + scatter + gather

    def copies(self):
        return 2 * self.tensor_copies() + self.n_ada - 1 + self.n_avg - 1


def chunk_of(rows):
    return next(c for c in (32, 16, 8) if rows % c == 0)


def over_chunks(rows, body, init=0):
    size = chunk_of(rows)

    def step(i, carry):
        return body(pl.ds(pl.multiple_of(i * size, size), size), carry)

    return lax.fori_loop(0, rows // size, step, init)


def folded(block):
    return jnp.sum(block.reshape(block.shape[0] // 8, 8, block.shape[1]), axis=0)


def coefficients(dot, norm_a, norm_b):
    return (
        1.0 - dot / (2.0 * (norm_a + norm_eps)),
        1.0 - dot / (2.0 * (norm_b + norm_eps)),
    )


def comm_kernel(sz, *refs):
    g_first, g_second, g_vec, out_first, out_second, out_vec = refs[:6]
    scratch = refs[6:]
    per_first, per_second = scratch[:8], scratch[8:16]
    vec_ada, vec_avg, send, recv, local_sem = scratch[16:]

    me, v = lax.axis_index("ada"), lax.axis_index("avg")
    y, core = me // sz.core, me % sz.core
    z, x = v // sz.x, v % sz.x

    def ada_peer(a):
        return {"ada": a, "avg": v}

    def avg_peer(b):
        return {"ada": me, "avg": b}

    barrier = pltpu.get_barrier_semaphore()
    peers = [ada_peer(lax.rem(me + k, sz.n_ada)) for k in range(1, sz.n_ada)]
    peers += [avg_peer(lax.rem(v + k, sz.n_avg)) for k in range(1, sz.n_avg)]
    for peer in peers:
        pl.semaphore_signal(barrier, inc=1, device_id=peer, device_id_type=pl.DeviceIdType.MESH)
    pl.semaphore_wait(barrier, len(peers))

    started = []

    def start(src, dst, peer):
        i = len(started)
        copy = pltpu.make_async_remote_copy(
            src_ref=src, dst_ref=dst, send_sem=send.at[i], recv_sem=recv.at[i],
            device_id=peer, device_id_type=pl.DeviceIdType.MESH,
        )
        copy.start()
        started.append(copy)
        return copy

    def arrived(copies):
        for copy in copies:
            copy.wait_recv()

    vec_copies = []
    for k in range(1, sz.n_ada):
        peer = lax.rem(me + k, sz.n_ada)
        vec_copies.append(start(g_vec, vec_ada.at[me], ada_peer(peer)))
    slices = {}
    own_copies = {}
    for t, (grad, per) in enumerate(((g_second, per_second), (g_first, per_first))):
        got = per[0]
        part = grad.shape[0] // sz.n_ada
        own_copies[t] = pltpu.make_async_copy(
            grad.at[pl.ds(pl.multiple_of(me * part, 8), part)], got.at[me], local_sem.at[t]
        )
        own_copies[t].start()
        slices[t] = []
        order = [k for k in range(1, sz.n_ada) if k >= sz.core] + list(range(1, sz.core))
        for k in order:
            peer = jnp.bitwise_xor(me, k)
            rows = pl.ds(pl.multiple_of(peer * part, 8), part)
            slices[t].append(start(grad.at[rows], got.at[me], ada_peer(peer)))

    vec_ada[me] = g_vec[...]
    arrived(vec_copies)
    items = [vec_ada[a] for a in range(sz.n_ada)]
    while len(items) > 1:
        half = len(items) // 2
        merged = []
        for a, b in zip(items[:half], items[half:]):
            dot = jnp.sum(a * b, axis=1, keepdims=True)
            norm_a = jnp.sum(a * a, axis=1, keepdims=True)
            norm_b = jnp.sum(b * b, axis=1, keepdims=True)
            coef_a, coef_b = coefficients(dot, norm_a, norm_b)
            merged.append(coef_a * a + coef_b * b)
        items = merged
    vec_avg[v] = items[0]
    vec_out = []
    for k in range(1, sz.n_avg):
        peer = lax.rem(v + k, sz.n_avg)
        vec_out.append(start(vec_avg.at[v], vec_avg.at[v], avg_peer(peer)))

    def tensor(t, grad, out, per):
        got, stats, x_a, sum_a, z_a, z_b, sum_b, x_b = per
        part = grad.shape[0] // sz.n_ada
        strip = part // 2
        piece = strip // sz.z
        cols = sz.cols
        own_copies[t].wait()
        arrived(slices[t])

        def combine(level):
            half = sz.n_ada >> (level + 1)
            mine = stats.at[level, me]
            mine[...] = jnp.zeros((sz.stat_rows, sz.width), jnp.float32)
            for p in range(half):

                def add(rows, carry):
                    a, b = got[p, rows], got[p + half, rows]
                    return (
                        carry[0] + folded(a * b),
                        carry[1] + folded(a * a),
                        carry[2] + folded(b * b),
                    )

                zero = jnp.zeros((8, sz.width), jnp.float32)
                sums = over_chunks(part, add, (zero, zero, zero))
                for j, total in enumerate(sums):
                    row = 3 * p + j
                    mine[row : row + 1, :] = jnp.sum(total, axis=0, keepdims=True)
            copies = []
            for k in range(1, sz.n_ada):
                peer = lax.rem(me + k, sz.n_ada)
                copies.append(start(stats.at[level, me], stats.at[level, me], ada_peer(peer)))
            arrived(copies)
            total = stats[level, 0]
            for a in range(1, sz.n_ada):
                total = total + stats[level, a]
            total = jnp.sum(total, axis=1, keepdims=True)
            for p in range(half):
                coef_a, coef_b = coefficients(
                    total[3 * p : 3 * p + 1], total[3 * p + 1 : 3 * p + 2],
                    total[3 * p + 2 : 3 * p + 3],
                )

                def merge(rows, carry):
                    got[p, rows] = coef_a * got[p, rows] + coef_b * got[p + half, rows]
                    return carry

                over_chunks(part, merge)

        for level in range(sz.levels):
            combine(level)

        def at_x(i):
            return pl.ds(pl.multiple_of(i * cols, 128), cols)

        def at_z(i, base=0):
            return pl.ds(pl.multiple_of(base + i * piece, 8), piece)

        def z_peer(k):
            return lax.rem(z + k, sz.z)

        def x_peer(k):
            return lax.rem(x + k, sz.x)

        def z_dev(i):
            return avg_peer(i * sz.x + x)

        def x_dev(i):
            return avg_peer(z * sz.x + i)

        def total(rows, read, buffer, write):
            def body(window, carry):
                value = read(window)
                for k in range(buffer.shape[0]):
                    value = value + buffer[k, window]
                write(window, value)
                return carry

            over_chunks(rows, body)

        def shifted(window, base):
            return pl.ds(pl.multiple_of(base + window.start, 8), window.size)

        whole = got.at[0]
        a_x = [
            start(whole.at[pl.ds(0, strip), at_x(x_peer(k))], x_a.at[k - 1], x_dev(x_peer(k)))
            for k in range(1, sz.x)
        ]
        b_z = [
            start(whole.at[at_z(z_peer(k), strip)], z_b.at[k - 1], z_dev(z_peer(k)))
            for k in range(1, sz.z)
        ]

        def put(ref):
            def write(window, value):
                ref[window] = value

            return write

        def put_out(base):
            def write(window, value):
                out[shifted(window, base), at_x(x)] = value

            return write

        arrived(a_x)
        total(strip, lambda w: got[0, w, at_x(x)], x_a, put(sum_a))
        a_z = [
            start(sum_a.at[at_z(z_peer(k))], z_a.at[k - 1], z_dev(z_peer(k)))
            for k in range(1, sz.z)
        ]
        arrived(b_z)
        total(piece, lambda w: got[0, shifted(w, strip + z * piece)], z_b, put(sum_b))
        b_x = [
            start(sum_b.at[:, at_x(x_peer(k))], x_b.at[k - 1], x_dev(x_peer(k)))
            for k in range(1, sz.x)
        ]

        def base_of(side, row_y):
            return (row_y * sz.core + core) * part + side * strip

        def spread(side, row_y, columns, peer):
            rows = pl.ds(pl.multiple_of(base_of(side, row_y), 8), strip)
            block = out.at[rows] if columns is None else out.at[rows, columns]
            return start(block, block, peer)

        def spread_z(side):
            block = out.at[at_z(z, base_of(side, y)), at_x(x)]
            return [start(block, block, z_dev(z_peer(k))) for k in range(1, sz.z)]

        def y_row(k):
            return lax.rem(y + k, sz.y)

        def spread_y(side, columns):
            return [
                spread(side, y, columns, ada_peer(y_row(k) * sz.core + core))
                for k in range(1, sz.y)
            ]

        def spread_x(side, row_y):
            return [spread(side, row_y, at_x(x), x_dev(x_peer(k))) for k in range(1, sz.x)]

        def spread_core(side, row_y):
            return [
                spread(side, row_y, None, ada_peer(y * sz.core + lax.rem(core + k, sz.core)))
                for k in range(1, sz.core)
            ]

        arrived(a_z)
        total(piece, lambda w: sum_a[shifted(w, z * piece)], z_a, put_out(base_of(0, y) + z * piece))
        a_gather = spread_z(0)
        arrived(b_x)
        total(piece, lambda w: sum_b[w, at_x(x)], x_b, put_out(base_of(1, y) + z * piece))
        b_gather = spread_z(1)

        arrived(a_gather)
        a_x = spread_x(0, y)
        arrived(b_gather)
        b_y = spread_y(1, at_x(x))
        b_x = spread_x(1, y)
        arrived(a_x)
        a_y = spread_y(0, None)
        last = spread_core(0, y)
        arrived(b_y)
        b_x_far = []
        for k in range(1, sz.y):
            b_x_far += spread_x(1, y_row(k))
        arrived(b_x)
        last += spread_core(1, y)
        arrived(a_y)
        for k in range(1, sz.y):
            last += spread_core(0, y_row(k))
        arrived(b_x_far)
        for k in range(1, sz.y):
            last += spread_core(1, y_row(k))
        return last

    last = tensor(0, g_second, out_second, per_second)
    arrived(vec_out)
    vec_total = vec_avg[0]
    for b in range(1, sz.n_avg):
        vec_total = vec_total + vec_avg[b]
    out_vec[...] = vec_total
    last += tensor(1, g_first, out_first, per_first)
    arrived(last)
    for copy in started:
        copy.wait_send()


def tensor_scratch(sz, rows):
    part = rows // sz.n_ada
    strip = part // 2
    piece = strip // sz.z

    def vmem(*shape):
        return pltpu.VMEM(shape, jnp.float32)

    return [
        vmem(sz.n_ada, part, sz.width),
        vmem(sz.levels, sz.n_ada, sz.stat_rows, sz.width),
        vmem(max(sz.x - 1, 1), strip, sz.cols),
        vmem(strip, sz.cols),
        vmem(max(sz.z - 1, 1), piece, sz.cols),
        vmem(max(sz.z - 1, 1), piece, sz.width),
        vmem(piece, sz.width),
        vmem(max(sz.x - 1, 1), piece, sz.cols),
    ]


def adasum_totals(first, second, vectors):
    sz = Sizes(lax.axis_size("ada"), lax.axis_size("avg"), first.shape[1])
    in_vmem = pl.BlockSpec(memory_space=pltpu.VMEM)
    anywhere = pl.BlockSpec(memory_space=pl.ANY)
    return pl.pallas_call(
        functools.partial(comm_kernel, sz),
        out_shape=[jax.ShapeDtypeStruct(a.shape, a.dtype) for a in (first, second, vectors)],
        in_specs=[anywhere, anywhere, in_vmem],
        out_specs=[in_vmem] * 3,
        scratch_shapes=tensor_scratch(sz, first.shape[0])
        + tensor_scratch(sz, second.shape[0])
        + [
            pltpu.VMEM((sz.n_ada,) + vectors.shape, jnp.float32),
            pltpu.VMEM((sz.n_avg,) + vectors.shape, jnp.float32),
            pltpu.SemaphoreType.DMA((sz.copies(),)),
            pltpu.SemaphoreType.DMA((sz.copies(),)),
            pltpu.SemaphoreType.DMA((2,)),
        ],
        compiler_params=pltpu.CompilerParams(
            collective_id=0, has_side_effects=True, vmem_limit_bytes=40 * 2**20
        ),
        name="adasum_totals",
    )(first, second, vectors)


def local(edges, teacher, w_first, b_first, w_second, b_second, norm_gain, norm_shift):
    params = (w_first, b_first, w_second, b_second, norm_gain, norm_shift)
    grads = jax.grad(local_loss)(params, edges, teacher)
    vectors = jnp.stack([grads[1], grads[3], grads[4], grads[5]])
    vectors = jnp.concatenate([vectors, jnp.zeros_like(vectors)], axis=0)
    first, second, vec = adasum_totals(grads[0], grads[2], vectors)
    avg_count = lax.axis_size("avg")

    def new(param, total):
        return param - step_rate * (total / avg_count)

    return (
        new(w_first, first),
        new(b_first, vec[0]),
        new(w_second, second),
        new(b_second, vec[1]),
        new(norm_gain, vec[2]),
        new(norm_shift, vec[3]),
    )


def solution(mesh):
    in_specs = (P(("ada", "avg"), None), P(("ada", "avg"), None), P(), P(), P(), P(), P(), P())
    out_specs = (P(), P(), P(), P(), P(), P())
    return jax.shard_map(local, mesh=mesh, in_specs=in_specs, out_specs=out_specs, check_vma=False)
```

time: 316 us -> 182 us (0.58)
  waiting for transfers between devices: 134 us -> 0 us
  Pallas kernels: 0 us -> 121 us
  other arithmetic: 46.1 us -> 11.6 us
  blocking collectives: 25.4 us -> 0 us
  matrix products: 62.2 us -> 41.3 us
  local copies, waits for them, and re-layouts: 18.2 us -> 4.27 us
  between operations: 14.5 us -> 0.78 us
  starting transfers between devices: 9.85 us -> 0 us
    pallas_call x0 -> x1, Pallas kernels: none -> 121 us  [adasum_totals(): pl.pallas_call(functools.partial(comm_kernel, sz), out_shape=[jax.ShapeDt...]
    psum x1 -> x0, waiting for transfers between devices: 79.9 us -> none  [local(): sums = lax.psum((pieces[0], pieces[1], pieces[2]), 'avg')]
    ppermute x9 -> x0, waiting for transfers between devices: 38.6 us -> none  [swapped(): return lax.ppermute(block, axis, route)]
    dot_general x5, matrix products: 62.2 us -> 41.3 us  [the longest x2 23.3 us: local_loss(): jnp.dot(inputs, w_first, precision=prec, preferred_element_type=jnp.float32)]
    psum x1 -> x0, blocking collectives: 20.1 us -> none  [local(): sums = lax.psum((pieces[0], pieces[1], pieces[2]), 'avg')]
    all_gather x2 -> x0, waiting for transfers between devices: 15.4 us -> none  [the longest x1 15.4 us: local(): lax.all_gather(updated[0], 'ada', axis=0, tiled=True)]
    reduce_sum x7 -> x1, other arithmetic: 12.6 us -> 0.29 us  [local_loss(): jnp.dot(hidden, w_second, precision=prec, preferred_element_type=jnp.floa...]
    add x9 -> x0, other arithmetic: 12.3 us -> none  [the longest x2 6.54 us: local(): coef_mine[0] * kept[0] + coef_other[0] * got[0]]
  transfers between devices with their start and end apart: 12 -> 0, of which waited for: 7 -> 0; matrix products, arithmetic and copies ran while one was open for 10% -> 0% of each run, Pallas kernels for 0% -> 0%
where the time goes in v1:
time: 182 us; the launch traced here: 179 us
  Pallas kernels  121 us (66%)
  matrix products  41.3 us (23%)
  other arithmetic  11.6 us (6%)
  local copies, waits for them, and re-layouts  4.27 us (2%)
    pallas_call x1, Pallas kernels, adasum_totals(): pl.pallas_call(functools.partial(comm_kernel, sz), out_shape=[jax.ShapeDt...  121 us
    dot_general x2, matrix products, local_loss(): jnp.dot(inputs, w_first, precision=prec, preferred_element_type=jnp.float32)  23.3 us
    dot_general x3, matrix products, local_loss(): jnp.dot(hidden, w_second, precision=prec, preferred_element_type=jnp.floa...  18 us
    sub x6, other arithmetic, new(): return param - step_rate * (total / avg_count)  5.94 us
    unnamed x15, local copies, waits for them, and re-layouts  4.24 us

profile of v1, /device:TPU:0, one launch (start us, length us, event | category | flops | bytes accessed | tf_op | source)
XLA Modules:
  0.0 179.2 jit_solution(9775484807807493185)
XLA Ops:
  0.6 0.7 broadcast_multiply_fusion.1
  1.3 12.2 %convolution_add_fusion.1 = f32[1536,512]{1,0:T(8,128)} fusion(f32[1536,1536]{1,0:T(8,128)} %param.8, f32[1536,512]{1,0:T(8,128)} %param.10, f32[512]{0:T(512)} %param.11), kind=kOutput, calls=%fused_computation.4 | convolution fusion | flops 7248543744 | bytes 15730688 | tf_op jit(solution)/shard_map/jvp()/dot_general | solution.py:17
  13.5 2.4 %copy.14 = f32[1536,512]{0,1:T(8,128)S(1)} copy(f32[1536,512]{1,0:T(8,128)} %param.9) | data formatting | bytes 6291456 | tf_op args[1]
  15.9 5.2 %fusion.17 = (f32[1536]{0:T(1024)S(1)}, f32[1536,512]{0,1:T(8,128)S(1)}) fusion(f32[512]{0:T(512)S(1)} %copy-done.4, f32[512,512]{1,0:T(8,128)} %param.12, f32[1536,512]{1,0:T(8,128)} %convolution_add_fusion.1), kind=kOutput, calls=%fused_computation.36 | convolution fusion | flops 2420636160 | bytes 7348224 | tf_op jit(solution)/shard_map/jvp()/dot_general | solution.py:20
  21.1 0.0 copy-start.2
  21.1 0.0 copy-start.3
  21.2 0.4 multiply_reduce_fusion.2
  21.6 0.2 copy-done.2
  21.8 0.0 copy-done.3
  21.8 2.7 %multiply_reduce_fusion.3 = (f32[512]{0:T(512)S(1)}, f32[512]{0:T(512)S(1)}, f32[1536]{0:T(1024)S(1)}) fusion(f32[1536,512]{0,1:T(8,128)S(1)} %copy.14, f32[512]{0:T(512)S(1)} %copy-done.3, f32[512]{0:T(512)S(1)} %copy-done.2, f32[1536]{0:T(1024)S(1)} %fusion.13, f32[1536,512]{0,1:T(8,128)S(1)} %get-tuple-element.22, f32[1536]{0:T(1024)S(1)} %broadcast_multiply_fusion, ...), kind=kLoop, calls=%fused_computation.14 | loop fusion | flops 9434624 | bytes 6320128 | tf_op jit(solution)/shard_map/transpose(jvp())/reduce_sum | solution.py:24
  24.6 1.5 fusion.16
  26.1 0.3 add_reduce_fusion
  26.4 1.6 copy-done.6
  28.0 5.2 %fusion.3.refs_1_ = f32[512,512]{1,0:T(8,128)S(1)} fusion(f32[1536,512]{0,1:T(8,128)S(1)} %get-tuple-element.16, f32[1536]{0:T(1024)S(1)} %negate_multiply_fusion, f32[1536,512]{1,0:T(8,128)S(1)} %copy-done.6), kind=kOutput, calls=%fused_computation.16 | convolution fusion | flops 2419851264 | bytes 7346176 | tf_op jit(solution)/shard_map/transpose(jvp())/dot_general | solution.py:20
  33.2 7.6 %fusion.18 = (f32[512]{0:T(512)S(1)}, f32[1536,512]{1,0:T(8,128)}) fusion(f32[1536,512]{1,0:T(8,128)S(1)} %copy-done.6, f32[512,512]{1,0:T(8,128)S(1)} %copy-done.1, f32[1536,512]{0,1:T(8,128)S(1)} %get-tuple-element.16, f32[1536]{0:T(1024)S(1)} %negate_multiply_fusion), kind=kOutput, calls=%fused_computation.37 | convolution fusion | flops 2424569344 | bytes 10493952 | tf_op jit(solution)/shard_map/transpose(jvp())/dot_general | solution.py:20
  40.8 11.1 %convolution_bitcast_fusion.refs_0_ = f32[1536,512]{1,0:T(8,128)S(1)} fusion(f32[1536,512]{1,0:T(8,128)} %get-tuple-element.24, f32[1536,1536]{1,0:T(8,128)} %param.8), kind=kOutput, calls=%fused_computation.3 | convolution fusion | flops 7247757312 | bytes 15728640 | tf_op jit(solution)/shard_map/transpose(jvp())/dot_general | solution.py:17
  51.9 0.0 copy-start
  51.9 121.2 %adasum_totals.1 = (f32[1536,512]{1,0:T(8,128)S(1)}, f32[512,512]{1,0:T(8,128)S(1)}, f32[8,512]{1,0:T(8,128)S(1)}) custom-call(f32[1536,512]{1,0:T(8,128)S(1)} %convolution_bitcast_fusion.refs_0_, f32[512,512]{1,0:T(8,128)S(1)} %fusion.3.refs_1_, f32[8,512]{1,0:T(8,128)S(1)} %concatenate.3.refs_2_), custom_call_target="tpu_custom_call" | custom-call | tf_op jit(solution)/shard_map/adasum_totals/pallas_call | solution.py:364
  173.2 2.4 %multiply_subtract_fusion = f32[1536,512]{1,0:T(8,128)} fusion(f32[1536,512]{1,0:T(8,128)S(1)} %copy-done, f32[1536,512]{1,0:T(8,128)S(1)} %get-tuple-element.9), kind=kLoop, calls=%fused_computation.7 | loop fusion | flops 1572864 | bytes 9437184 | tf_op jit(solution)/shard_map/sub | solution.py:394
  175.7 0.6 sub.41
  176.2 0.6 sub.40
  176.8 0.6 sub.39
  177.4 0.6 sub.37
  178.0 1.2 multiply_subtract_fusion.1
  (15 shorter events, 0.1 us)
Async XLA Ops:
  13.5 2.4 %copy-start.4 = (f32[512]{0:T(512)S(1)}, f32[512]{0:T(512)}, u32[]{:S(2)}) copy-start(f32[512]{0:T(512)} %param.13) | copy-start | bytes 6148
  21.1 0.7 copy-start.2
  21.1 0.7 copy-start.3
  26.1 1.9 %copy-start.6 = (f32[1536,512]{1,0:T(8,128)S(1)}, f32[1536,512]{1,0:T(8,128)}, u32[]{:S(2)}) copy-start(f32[1536,512]{1,0:T(8,128)} %convolution_add_fusion.1) | copy-start | bytes 9437188
  28.0 5.2 %copy-start.1 = (f32[512,512]{1,0:T(8,128)S(1)}, f32[512,512]{1,0:T(8,128)}, u32[]{:S(2)}) copy-start(f32[512,512]{1,0:T(8,128)} %param.12) | copy-start | bytes 3145732
  51.9 121.3 %copy-start = (f32[1536,512]{1,0:T(8,128)S(1)}, f32[1536,512]{1,0:T(8,128)}, u32[]{:S(2)}) copy-start(f32[1536,512]{1,0:T(8,128)} %param.10) | copy-start | bytes 9437188
  173.2 4.2 %copy-start.5 = (f32[512]{0:T(512)S(1)}, f32[512]{0:T(512)}, u32[]{:S(2)}) copy-start(f32[512]{0:T(512)} %param.11) | copy-start | bytes 6148

commit v2 on v1

--- a/solution.py
+++ b/solution.py
@@ -33,14 +33,13 @@
         self.x = self.y if n_avg % self.y == 0 else 1
         self.z = n_avg // self.x
         self.cols = width // self.x
-        self.levels = n_ada.bit_length() - 1
-        self.stat_rows = -(-3 * (n_ada // 2) // 8) * 8
+        self.stat_rows = -(-(n_ada * (n_ada + 1) // 2) // 8) * 8
 
     def tensor_copies(self):
         gather = 2 * (self.z - 1) + self.x - 1 + 2 * (self.y - 1) + self.y * (self.x - 1)
         gather += 2 * self.y * (self.core - 1)
         scatter = 2 * (self.x - 1) + 2 * (self.z - 1)
-        return (1 + self.levels) * (self.n_ada - 1) + scatter + gather
+        return 2 * (self.n_ada - 1) + scatter + gather
 
     def copies(self):
         return 2 * self.tensor_copies() + self.n_ada - 1 + self.n_avg - 1
@@ -50,8 +49,8 @@
     return next(c for c in (32, 16, 8) if rows % c == 0)
 
 
-def over_chunks(rows, body, init=0):
-    size = chunk_of(rows)
+def over_chunks(rows, body, init=0, size=None):
+    size = size or chunk_of(rows)
 
     def step(i, carry):
         return body(pl.ds(pl.multiple_of(i * size, size), size), carry)
@@ -68,6 +67,32 @@
         1.0 - dot / (2.0 * (norm_a + norm_eps)),
         1.0 - dot / (2.0 * (norm_b + norm_eps)),
     )
+
+
+def adasum_weights(inner, count):
+    def product(i, j):
+        return inner[min(i, j), max(i, j)]
+
+    weights = [{a: jnp.ones((1, 1), jnp.float32)} for a in range(count)]
+    while count > 1:
+        half = count // 2
+        coefs = [
+            coefficients(product(p, p + half), product(p, p), product(p + half, p + half))
+            for p in range(half)
+        ]
+        merged, following = [], {}
+        for p in range(half):
+            both = {a: coefs[p][0] * w for a, w in weights[p].items()}
+            both.update({a: coefs[p][1] * w for a, w in weights[p + half].items()})
+            merged.append(both)
+            for q in range(p, half):
+                value = 0.0
+                for i, left in zip((p, p + half), coefs[p]):
+                    for j, right in zip((q, q + half), coefs[q]):
+                        value = value + left * right * product(i, j)
+                following[p, q] = jnp.maximum(value, 0.0) if p == q else value
+        weights, inner, count = merged, following, half
+    return [weights[0][a] for a in sorted(weights[0])]
 
 
 def comm_kernel(sz, *refs):
@@ -113,21 +138,29 @@
     for k in range(1, sz.n_ada):
         peer = lax.rem(me + k, sz.n_ada)
         vec_copies.append(start(g_vec, vec_ada.at[me], ada_peer(peer)))
-    slices = {}
-    own_copies = {}
-    for t, (grad, per) in enumerate(((g_second, per_second), (g_first, per_first))):
-        got = per[0]
+    sides = ((g_second, per_second), (g_first, per_first))
+    own_copies = []
+    slices = ([], [])
+    for t, (grad, per) in enumerate(sides):
         part = grad.shape[0] // sz.n_ada
-        own_copies[t] = pltpu.make_async_copy(
-            grad.at[pl.ds(pl.multiple_of(me * part, 8), part)], got.at[me], local_sem.at[t]
+        rows = pl.ds(pl.multiple_of(me * part, 8), part)
+        own_copies.append(
+            pltpu.make_async_copy(grad.at[rows], per[0].at[me], local_sem.at[t])
         )
         own_copies[t].start()
-        slices[t] = []
-        order = [k for k in range(1, sz.n_ada) if k >= sz.core] + list(range(1, sz.core))
-        for k in order:
+
+    def give(t, offsets):
+        grad, per = sides[t]
+        part = grad.shape[0] // sz.n_ada
+        for k in offsets:
             peer = jnp.bitwise_xor(me, k)
             rows = pl.ds(pl.multiple_of(peer * part, 8), part)
-            slices[t].append(start(grad.at[rows], got.at[me], ada_peer(peer)))
+            slices[t].append(start(grad.at[rows], per[0].at[me], ada_peer(peer)))
+
+    far, near = list(range(sz.core, sz.n_ada)), list(range(1, sz.core))
+    cut = len(far) // 2
+    give(0, far + near)
+    give(1, far[:cut] + near)
 
     vec_ada[me] = g_vec[...]
     arrived(vec_copies)
@@ -157,48 +190,42 @@
         own_copies[t].wait()
         arrived(slices[t])
 
-        def combine(level):
-            half = sz.n_ada >> (level + 1)
-            mine = stats.at[level, me]
-            mine[...] = jnp.zeros((sz.stat_rows, sz.width), jnp.float32)
-            for p in range(half):
-
-                def add(rows, carry):
-                    a, b = got[p, rows], got[p + half, rows]
-                    return (
-                        carry[0] + folded(a * b),
-                        carry[1] + folded(a * a),
-                        carry[2] + folded(b * b),
-                    )
-
-                zero = jnp.zeros((8, sz.width), jnp.float32)
-                sums = over_chunks(part, add, (zero, zero, zero))
-                for j, total in enumerate(sums):
-                    row = 3 * p + j
-                    mine[row : row + 1, :] = jnp.sum(total, axis=0, keepdims=True)
-            copies = []
-            for k in range(1, sz.n_ada):
-                peer = lax.rem(me + k, sz.n_ada)
-                copies.append(start(stats.at[level, me], stats.at[level, me], ada_peer(peer)))
-            arrived(copies)
-            total = stats[level, 0]
+        pairs = [(i, j) for i in range(sz.n_ada) for j in range(i, sz.n_ada)]
+        mine = stats.at[me]
+        mine[...] = jnp.zeros((sz.stat_rows, sz.width), jnp.float32)
+        for some in (pairs[i : i + 5] for i in range(0, len(pairs), 5)):
+
+            def add(rows, carry):
+                used = {i: got[i, rows] for pair in some for i in pair}
+                return tuple(c + folded(used[i] * used[j]) for c, (i, j) in zip(carry, some))
+
+            zero = jnp.zeros((8, sz.width), jnp.float32)
+            sums = over_chunks(part, add, (zero,) * len(some), 8)
+            for pair, value in zip(some, sums):
+                row = pairs.index(pair)
+                mine[row : row + 1, :] = jnp.sum(value, axis=0, keepdims=True)
+        stat_copies = []
+        for k in range(1, sz.n_ada):
+            peer = lax.rem(me + k, sz.n_ada)
+            stat_copies.append(start(stats.at[me], stats.at[me], ada_peer(peer)))
+        yield
+        arrived(stat_copies)
+        gathered = stats[0]
+        for a in range(1, sz.n_ada):
+            gathered = gathered + stats[a]
+        gathered = jnp.sum(gathered, axis=1, keepdims=True)
+        weights = adasum_weights(
+            {pair: gathered[row : row + 1] for row, pair in enumerate(pairs)}, sz.n_ada
+        )
+
+        def merge(rows, carry):
+            value = weights[0] * got[0, rows]
             for a in range(1, sz.n_ada):
-                total = total + stats[level, a]
-            total = jnp.sum(total, axis=1, keepdims=True)
-            for p in range(half):
-                coef_a, coef_b = coefficients(
-                    total[3 * p : 3 * p + 1], total[3 * p + 1 : 3 * p + 2],
-                    total[3 * p + 2 : 3 * p + 3],
-                )
-
-                def merge(rows, carry):
-                    got[p, rows] = coef_a * got[p, rows] + coef_b * got[p + half, rows]
-                    return carry
-
-                over_chunks(part, merge)
-
-        for level in range(sz.levels):
-            combine(level)
+                value = value + weights[a] * got[a, rows]
+            got[0, rows] = value
+            return carry
+
+        over_chunks(part, merge)
 
         def at_x(i):
             return pl.ds(pl.multiple_of(i * cols, 128), cols)
@@ -253,12 +280,14 @@
 
             return write
 
+        yield
         arrived(a_x)
         total(strip, lambda w: got[0, w, at_x(x)], x_a, put(sum_a))
         a_z = [
             start(sum_a.at[at_z(z_peer(k))], z_a.at[k - 1], z_dev(z_peer(k)))
             for k in range(1, sz.z)
         ]
+        yield
         arrived(b_z)
         total(piece, lambda w: got[0, shifted(w, strip + z * piece)], z_b, put(sum_b))
         b_x = [
@@ -296,43 +325,60 @@
                 for k in range(1, sz.core)
             ]
 
+        yield
         arrived(a_z)
         total(piece, lambda w: sum_a[shifted(w, z * piece)], z_a, put_out(base_of(0, y) + z * piece))
         a_gather = spread_z(0)
+        yield
         arrived(b_x)
         total(piece, lambda w: sum_b[w, at_x(x)], x_b, put_out(base_of(1, y) + z * piece))
         b_gather = spread_z(1)
 
+        yield
         arrived(a_gather)
         a_x = spread_x(0, y)
+        yield
         arrived(b_gather)
         b_y = spread_y(1, at_x(x))
         b_x = spread_x(1, y)
+        yield
         arrived(a_x)
         a_y = spread_y(0, None)
         last = spread_core(0, y)
+        yield
         arrived(b_y)
         b_x_far = []
         for k in range(1, sz.y):
             b_x_far += spread_x(1, y_row(k))
+        yield
         arrived(b_x)
         last += spread_core(1, y)
+        yield
         arrived(a_y)
         for k in range(1, sz.y):
             last += spread_core(0, y_row(k))
+        yield
         arrived(b_x_far)
         for k in range(1, sz.y):
             last += spread_core(1, y_row(k))
-        return last
-
-    last = tensor(0, g_second, out_second, per_second)
+        yield
+        arrived(last)
+
+    second = tensor(0, g_second, out_second, per_second)
+    first = tensor(1, g_first, out_first, per_first)
+    next(second)
+    give(1, far[cut:])
+    for _ in range(5):
+        next(second)
     arrived(vec_out)
     vec_total = vec_avg[0]
     for b in range(1, sz.n_avg):
         vec_total = vec_total + vec_avg[b]
     out_vec[...] = vec_total
-    last += tensor(1, g_first, out_first, per_first)
-    arrived(last)
+    running = [first, second]
+    while running:
+        running = [one for one in running if next(one, True) is None]
+
     for copy in started:
         copy.wait_send()
 
@@ -347,7 +393,7 @@
 
     return [
         vmem(sz.n_ada, part, sz.width),
-        vmem(sz.levels, sz.n_ada, sz.stat_rows, sz.width),
+        vmem(sz.n_ada, sz.stat_rows, sz.width),
         vmem(max(sz.x - 1, 1), strip, sz.cols),
         vmem(strip, sz.cols),
         vmem(max(sz.z - 1, 1), piece, sz.cols),

time: 182 us -> 157 us (0.86)
  Pallas kernels: 121 us -> 97.7 us
    pallas_call x1, Pallas kernels: 121 us -> 97.7 us  [adasum_totals(): pl.pallas_call(functools.partial(comm_kernel, sz), out_shape=[jax.ShapeDt...]
where the time goes in v2:
time: 157 us; the launch traced here: 156 us
  Pallas kernels  97.7 us (62%)
  matrix products  41.3 us (26%)
  other arithmetic  11.6 us (7%)
  local copies, waits for them, and re-layouts  4.27 us (3%)
    pallas_call x1, Pallas kernels, adasum_totals(): pl.pallas_call(functools.partial(comm_kernel, sz), out_shape=[jax.ShapeDt...  97.7 us
    dot_general x2, matrix products, local_loss(): jnp.dot(inputs, w_first, precision=prec, preferred_element_type=jnp.float32)  23.3 us
    dot_general x3, matrix products, local_loss(): jnp.dot(hidden, w_second, precision=prec, preferred_element_type=jnp.floa...  18 us
    sub x6, other arithmetic, new(): return param - step_rate * (total / avg_count)  5.94 us
    unnamed x15, local copies, waits for them, and re-layouts  4.24 us

profile of v2, /device:TPU:0, one launch (start us, length us, event | category | flops | bytes accessed | tf_op | source)
XLA Modules:
  0.0 155.6 jit_solution(5596961175006224892)
XLA Ops:
  0.6 0.7 broadcast_multiply_fusion.1
  1.3 12.2 %convolution_add_fusion.1 = f32[1536,512]{1,0:T(8,128)} fusion(f32[1536,1536]{1,0:T(8,128)} %param.8, f32[1536,512]{1,0:T(8,128)} %param.10, f32[512]{0:T(512)} %param.11), kind=kOutput, calls=%fused_computation.4 | convolution fusion | flops 7248543744 | bytes 15730688 | tf_op jit(solution)/shard_map/jvp()/dot_general | solution.py:17
  13.5 2.4 %copy.14 = f32[1536,512]{0,1:T(8,128)S(1)} copy(f32[1536,512]{1,0:T(8,128)} %param.9) | data formatting | bytes 6291456 | tf_op args[1]
  15.9 5.2 %fusion.17 = (f32[1536]{0:T(1024)S(1)}, f32[1536,512]{0,1:T(8,128)S(1)}) fusion(f32[512]{0:T(512)S(1)} %copy-done.4, f32[512,512]{1,0:T(8,128)} %param.12, f32[1536,512]{1,0:T(8,128)} %convolution_add_fusion.1), kind=kOutput, calls=%fused_computation.36 | convolution fusion | flops 2420636160 | bytes 7348224 | tf_op jit(solution)/shard_map/jvp()/dot_general | solution.py:20
  21.1 0.0 copy-start.3
  21.2 0.4 multiply_reduce_fusion.2
  21.6 0.2 copy-done.2
  21.8 0.0 copy-done.3
  21.8 2.7 %multiply_reduce_fusion.3 = (f32[512]{0:T(512)S(1)}, f32[512]{0:T(512)S(1)}, f32[1536]{0:T(1024)S(1)}) fusion(f32[1536,512]{0,1:T(8,128)S(1)} %copy.14, f32[512]{0:T(512)S(1)} %copy-done.3, f32[512]{0:T(512)S(1)} %copy-done.2, f32[1536]{0:T(1024)S(1)} %fusion.13, f32[1536,512]{0,1:T(8,128)S(1)} %get-tuple-element.22, f32[1536]{0:T(1024)S(1)} %broadcast_multiply_fusion, ...), kind=kLoop, calls=%fused_computation.14 | loop fusion | flops 9434624 | bytes 6320128 | tf_op jit(solution)/shard_map/transpose(jvp())/reduce_sum | solution.py:24
  24.6 1.5 fusion.16
  26.1 0.0 copy-start.6
  26.1 0.3 add_reduce_fusion
  26.4 1.6 %copy-done.6 = f32[1536,512]{1,0:T(8,128)S(1)} copy-done((f32[1536,512]{1,0:T(8,128)S(1)}, f32[1536,512]{1,0:T(8,128)}, u32[]{:S(2)}) %copy-start.6) | copy-done | bytes 3145752
  28.0 5.2 %fusion.3.refs_1_ = f32[512,512]{1,0:T(8,128)S(1)} fusion(f32[1536,512]{0,1:T(8,128)S(1)} %get-tuple-element.16, f32[1536]{0:T(1024)S(1)} %negate_multiply_fusion, f32[1536,512]{1,0:T(8,128)S(1)} %copy-done.6), kind=kOutput, calls=%fused_computation.16 | convolution fusion | flops 2419851264 | bytes 7346176 | tf_op jit(solution)/shard_map/transpose(jvp())/dot_general | solution.py:20
  33.2 7.6 %fusion.18 = (f32[512]{0:T(512)S(1)}, f32[1536,512]{1,0:T(8,128)}) fusion(f32[1536,512]{1,0:T(8,128)S(1)} %copy-done.6, f32[512,512]{1,0:T(8,128)S(1)} %copy-done.1, f32[1536,512]{0,1:T(8,128)S(1)} %get-tuple-element.16, f32[1536]{0:T(1024)S(1)} %negate_multiply_fusion), kind=kOutput, calls=%fused_computation.37 | convolution fusion | flops 2424569344 | bytes 10493952 | tf_op jit(solution)/shard_map/transpose(jvp())/dot_general | solution.py:20
  40.8 11.1 %convolution_bitcast_fusion.refs_0_ = f32[1536,512]{1,0:T(8,128)S(1)} fusion(f32[1536,512]{1,0:T(8,128)} %get-tuple-element.24, f32[1536,1536]{1,0:T(8,128)} %param.8), kind=kOutput, calls=%fused_computation.3 | convolution fusion | flops 7247757312 | bytes 15728640 | tf_op jit(solution)/shard_map/transpose(jvp())/dot_general | solution.py:17
  51.9 97.7 %adasum_totals.1 = (f32[1536,512]{1,0:T(8,128)S(1)}, f32[512,512]{1,0:T(8,128)S(1)}, f32[8,512]{1,0:T(8,128)S(1)}) custom-call(f32[1536,512]{1,0:T(8,128)S(1)} %convolution_bitcast_fusion.refs_0_, f32[512,512]{1,0:T(8,128)S(1)} %fusion.3.refs_1_, f32[8,512]{1,0:T(8,128)S(1)} %concatenate.3.refs_2_), custom_call_target="tpu_custom_call" | custom-call | tf_op jit(solution)/shard_map/adasum_totals/pallas_call | solution.py:410
  149.6 0.0 copy-start.5
  149.7 2.4 %multiply_subtract_fusion = f32[1536,512]{1,0:T(8,128)} fusion(f32[1536,512]{1,0:T(8,128)S(1)} %copy-done, f32[1536,512]{1,0:T(8,128)S(1)} %get-tuple-element.9), kind=kLoop, calls=%fused_computation.7 | loop fusion | flops 1572864 | bytes 9437184 | tf_op jit(solution)/shard_map/sub | solution.py:440
  152.1 0.6 sub.41
  152.7 0.6 sub.40
  153.3 0.6 sub.39
  153.8 0.6 sub.37
  154.4 1.2 multiply_subtract_fusion.1
  (15 shorter events, 0.1 us)
Async XLA Ops:
  13.5 2.4 %copy-start.4 = (f32[512]{0:T(512)S(1)}, f32[512]{0:T(512)}, u32[]{:S(2)}) copy-start(f32[512]{0:T(512)} %param.13) | copy-start | bytes 6148
  21.1 0.7 copy-start.2
  21.1 0.7 copy-start.3
  26.1 1.9 %copy-start.6 = (f32[1536,512]{1,0:T(8,128)S(1)}, f32[1536,512]{1,0:T(8,128)}, u32[]{:S(2)}) copy-start(f32[1536,512]{1,0:T(8,128)} %convolution_add_fusion.1) | copy-start | bytes 9437188
  28.0 5.2 %copy-start.1 = (f32[512,512]{1,0:T(8,128)S(1)}, f32[512,512]{1,0:T(8,128)}, u32[]{:S(2)}) copy-start(f32[512,512]{1,0:T(8,128)} %param.12) | copy-start | bytes 3145732
  51.9 97.7 %copy-start = (f32[1536,512]{1,0:T(8,128)S(1)}, f32[1536,512]{1,0:T(8,128)}, u32[]{:S(2)}) copy-start(f32[1536,512]{1,0:T(8,128)} %param.10) | copy-start | bytes 9437188
  149.6 4.2 %copy-start.5 = (f32[512]{0:T(512)S(1)}, f32[512]{0:T(512)}, u32[]{:S(2)}) copy-start(f32[512]{0:T(512)} %param.11) | copy-start | bytes 6148

commit v3 on v2

--- a/solution.py
+++ b/solution.py
@@ -12,17 +12,16 @@
 prec = lax.Precision.HIGH
 
 
-def local_loss(params, inputs, targets):
-    w_first, b_first, w_second, b_second, norm_gain, norm_shift = params
-    zfirst = jnp.dot(inputs, w_first, precision=prec, preferred_element_type=jnp.float32) + b_first
-    hidden = zfirst * jax.nn.sigmoid(zfirst)
+def local_loss(params, first_sums, targets):
+    w_second, b_second, norm_gain, norm_shift = params
+    hidden = first_sums * jax.nn.sigmoid(first_sums)
     zsecond = (
         jnp.dot(hidden, w_second, precision=prec, preferred_element_type=jnp.float32) + b_second
     )
     center = zsecond - jnp.mean(zsecond, axis=1, keepdims=True)
     spread = jnp.mean(center * center, axis=1, keepdims=True)
     output = center * lax.rsqrt(spread + 1e-05) * norm_gain + norm_shift
-    return 0.5 * jnp.sum((output - targets) ** 2) / inputs.shape[0]
+    return 0.5 * jnp.sum((output - targets) ** 2) / first_sums.shape[0]
 
 
 class Sizes:
@@ -60,6 +59,17 @@
 
 def folded(block):
     return jnp.sum(block.reshape(block.shape[0] // 8, 8, block.shape[1]), axis=0)
+
+
+def split(value):
+    high = value.astype(jnp.bfloat16)
+    return high, (value - high.astype(jnp.float32)).astype(jnp.bfloat16)
+
+
+def contracted(left, right):
+    return lax.dot_general(
+        left, right, (((0,), (0,)), ((), ())), preferred_element_type=jnp.float32
+    )
 
 
 def coefficients(dot, norm_a, norm_b):
@@ -96,10 +106,11 @@
 
 
 def comm_kernel(sz, *refs):
-    g_first, g_second, g_vec, out_first, out_second, out_vec = refs[:6]
-    scratch = refs[6:]
+    x_ref, dz_ref, g_second, g_vec, out_first, out_second, out_vec = refs[:7]
+    scratch = refs[7:]
     per_first, per_second = scratch[:8], scratch[8:16]
-    vec_ada, vec_avg, send, recv, local_sem = scratch[16:]
+    vec_ada, vec_avg, send, recv, local_sem = scratch[16:21]
+    g_first, x_buf, dz_high, dz_low, x_sem = scratch[21:]
 
     me, v = lax.axis_index("ada"), lax.axis_index("avg")
     y, core = me // sz.core, me % sz.core
@@ -110,6 +121,32 @@
 
     def avg_peer(b):
         return {"ada": me, "avg": b}
+
+    sub = x_buf.shape[2]
+    chunk = x_ref.shape[1] // sz.y
+    firsts = [
+        jnp.bitwise_xor(y, k) * chunk + i * sub
+        for k in list(range(1, sz.y)) + [0]
+        for i in range(chunk // sub)
+    ]
+    loads = [
+        pltpu.make_async_copy(
+            x_ref.at[:, pl.ds(pl.multiple_of(first, 128), sub)],
+            x_buf.at[i % 2], x_sem.at[i % 2],
+        )
+        for i, first in enumerate(firsts)
+    ]
+    for load in loads[:2]:
+        load.start()
+
+    def weight_grad(i):
+        loads[i].wait()
+        high, low = split(x_buf[i % 2])
+        if i + 2 < len(loads):
+            loads[i + 2].start()
+        value = contracted(high, dz_low[...]) + contracted(low, dz_high[...])
+        rows = pl.ds(pl.multiple_of(firsts[i], 8), sub)
+        g_first[rows] = value + contracted(high, dz_high[...])
 
     barrier = pltpu.get_barrier_semaphore()
     peers = [ada_peer(lax.rem(me + k, sz.n_ada)) for k in range(1, sz.n_ada)]
@@ -147,7 +184,7 @@
         own_copies.append(
             pltpu.make_async_copy(grad.at[rows], per[0].at[me], local_sem.at[t])
         )
-        own_copies[t].start()
+    own_copies[0].start()
 
     def give(t, offsets):
         grad, per = sides[t]
@@ -160,7 +197,20 @@
     far, near = list(range(sz.core, sz.n_ada)), list(range(1, sz.core))
     cut = len(far) // 2
     give(0, far + near)
-    give(1, far[:cut] + near)
+
+    def split_rows(rows, carry):
+        dz_high[rows], dz_low[rows] = split(dz_ref[rows])
+        return carry
+
+    over_chunks(dz_ref.shape[0], split_rows)
+    away = len(loads) - chunk // sub
+    for i in range(away):
+        weight_grad(i)
+    give(1, far[:cut])
+    for i in range(away, len(loads)):
+        weight_grad(i)
+    give(1, near)
+    own_copies[1].start()
 
     vec_ada[me] = g_vec[...]
     arrived(vec_copies)
@@ -403,14 +453,18 @@
     ]
 
 
-def adasum_totals(first, second, vectors):
-    sz = Sizes(lax.axis_size("ada"), lax.axis_size("avg"), first.shape[1])
+def adasum_totals(edges, delta, second, vectors):
+    sz = Sizes(lax.axis_size("ada"), lax.axis_size("avg"), delta.shape[1])
+    rows, d_in = edges.shape
+    chunk = d_in // sz.y
+    sub = next(c for c in (384, 256, 128) if chunk % c == 0)
+    first = jax.ShapeDtypeStruct((d_in, delta.shape[1]), jnp.float32)
     in_vmem = pl.BlockSpec(memory_space=pltpu.VMEM)
     anywhere = pl.BlockSpec(memory_space=pl.ANY)
     return pl.pallas_call(
         functools.partial(comm_kernel, sz),
         out_shape=[jax.ShapeDtypeStruct(a.shape, a.dtype) for a in (first, second, vectors)],
-        in_specs=[anywhere, anywhere, in_vmem],
+        in_specs=[anywhere, in_vmem, anywhere, in_vmem],
         out_specs=[in_vmem] * 3,
         scratch_shapes=tensor_scratch(sz, first.shape[0])
         + tensor_scratch(sz, second.shape[0])
@@ -420,20 +474,28 @@
             pltpu.SemaphoreType.DMA((sz.copies(),)),
             pltpu.SemaphoreType.DMA((sz.copies(),)),
             pltpu.SemaphoreType.DMA((2,)),
+            pltpu.VMEM(first.shape, jnp.float32),
+            pltpu.VMEM((2, rows, sub), jnp.float32),
+            pltpu.VMEM(delta.shape, jnp.bfloat16),
+            pltpu.VMEM(delta.shape, jnp.bfloat16),
+            pltpu.SemaphoreType.DMA((2,)),
         ],
         compiler_params=pltpu.CompilerParams(
-            collective_id=0, has_side_effects=True, vmem_limit_bytes=40 * 2**20
+            collective_id=0, has_side_effects=True, vmem_limit_bytes=56 * 2**20
         ),
         name="adasum_totals",
-    )(first, second, vectors)
+    )(edges, delta, second, vectors)
 
 
 def local(edges, teacher, w_first, b_first, w_second, b_second, norm_gain, norm_shift):
-    params = (w_first, b_first, w_second, b_second, norm_gain, norm_shift)
-    grads = jax.grad(local_loss)(params, edges, teacher)
-    vectors = jnp.stack([grads[1], grads[3], grads[4], grads[5]])
+    first_sums = (
+        jnp.dot(edges, w_first, precision=prec, preferred_element_type=jnp.float32) + b_first
+    )
+    params = (w_second, b_second, norm_gain, norm_shift)
+    grads, delta = jax.grad(local_loss, argnums=(0, 1))(params, first_sums, teacher)
+    vectors = jnp.stack([jnp.sum(delta, axis=0), grads[1], grads[2], grads[3]])
     vectors = jnp.concatenate([vectors, jnp.zeros_like(vectors)], axis=0)
-    first, second, vec = adasum_totals(grads[0], grads[2], vectors)
+    first, second, vec = adasum_totals(edges, delta, grads[0], vectors)
     avg_count = lax.axis_size("avg")
 
     def new(param, total):

time: 157 us -> 154 us (0.981)
  matrix products: 41.3 us -> 31.2 us
  Pallas kernels: 97.7 us -> 102 us
  other arithmetic: 11.6 us -> 13.6 us
    dot_general x2 -> x1, matrix products: 23.3 us -> 12.2 us  [local(): jnp.dot(edges, w_first, precision=prec, preferred_element_type=jnp.float32)]
    pallas_call x1, Pallas kernels: 97.7 us -> 102 us  [adasum_totals(): pl.pallas_call(functools.partial(comm_kernel, sz), out_shape=[jax.ShapeDt...]
    sub x6, other arithmetic: 5.94 us -> 7.92 us  [new(): return param - step_rate * (total / avg_count)]
    unnamed x15 -> x19, local copies, waits for them, and re-layouts: 4.24 us -> 4.24 us
where the time goes in v3:
time: 154 us; the launch traced here: 152 us
  Pallas kernels  102 us (66%)
  matrix products  31.2 us (20%)
  other arithmetic  13.6 us (9%)
  local copies, waits for them, and re-layouts  4.86 us (3%)
    pallas_call x1, Pallas kernels, adasum_totals(): pl.pallas_call(functools.partial(comm_kernel, sz), out_shape=[jax.ShapeDt...  102 us
    dot_general x3, matrix products, local_loss(): jnp.dot(hidden, w_second, precision=prec, preferred_element_type=jnp.floa...  19 us
    dot_general x1, matrix products, local(): jnp.dot(edges, w_first, precision=prec, preferred_element_type=jnp.float32)  12.2 us
    sub x6, other arithmetic, new(): return param - step_rate * (total / avg_count)  7.92 us
    unnamed x19, local copies, waits for them, and re-layouts  4.24 us

profile of v3, /device:TPU:0, one launch (start us, length us, event | category | flops | bytes accessed | tf_op | source)
XLA Modules:
  0.0 152.0 jit_solution(11959408523209582038)
XLA Ops:
  0.6 0.7 broadcast_multiply_fusion.1
  1.3 12.2 %convolution_add_fusion.1 = f32[1536,512]{1,0:T(8,128)} fusion(f32[1536,1536]{1,0:T(8,128)} %refs_0_.1, f32[1536,512]{1,0:T(8,128)} %param.10, f32[512]{0:T(512)} %param.11), kind=kOutput, calls=%fused_computation.3 | convolution fusion | flops 7248543744 | bytes 15730688 | tf_op jit(solution)/shard_map/dot_general | solution.py:492
  13.5 2.4 %copy.14 = f32[1536,512]{0,1:T(8,128)S(1)} copy(f32[1536,512]{1,0:T(8,128)} %param.9) | data formatting | bytes 6291456 | tf_op args[1]
  15.9 5.2 %fusion.17 = (f32[1536]{0:T(1024)S(1)}, f32[1536,512]{0,1:T(8,128)S(1)}) fusion(f32[512]{0:T(512)S(1)} %copy-done.6, f32[512,512]{1,0:T(8,128)} %param.12, f32[1536,512]{1,0:T(8,128)} %convolution_add_fusion.1), kind=kOutput, calls=%fused_computation.35 | convolution fusion | flops 2420636160 | bytes 7348224 | tf_op jit(solution)/shard_map/jvp()/dot_general | solution.py:19
  21.1 0.0 copy-start.3
  21.1 0.0 copy-start.4
  21.2 0.4 multiply_reduce_fusion.2
  21.6 0.2 copy-done.3
  21.8 0.0 copy-done.4
  21.8 2.7 %multiply_reduce_fusion.3 = (f32[512]{0:T(512)S(1)}, f32[512]{0:T(512)S(1)}, f32[1536]{0:T(1024)S(1)}) fusion(f32[1536,512]{0,1:T(8,128)S(1)} %copy.14, f32[512]{0:T(512)S(1)} %copy-done.4, f32[512]{0:T(512)S(1)} %copy-done.3, f32[1536]{0:T(1024)S(1)} %fusion.13, f32[1536,512]{0,1:T(8,128)S(1)} %get-tuple-element.22, f32[1536]{0:T(1024)S(1)} %broadcast_multiply_fusion, ...), kind=kLoop, calls=%fused_computation.13 | loop fusion | flops 9434624 | bytes 6320128 | tf_op jit(solution)/shard_map/transpose(jvp())/reduce_sum | solution.py:23
  24.6 1.5 fusion.16
  26.1 0.0 copy-start.8
  26.1 0.3 add_reduce_fusion
  26.4 1.6 %copy-done.8 = f32[1536,512]{1,0:T(8,128)S(1)} copy-done((f32[1536,512]{1,0:T(8,128)S(1)}, f32[1536,512]{1,0:T(8,128)}, u32[]{:S(2)}) %copy-start.8) | copy-done | bytes 3145752
  28.0 6.2 %fusion.3.refs_2_ = f32[512,512]{1,0:T(8,128)} fusion(f32[1536,512]{0,1:T(8,128)S(1)} %get-tuple-element.16, f32[1536]{0:T(1024)S(1)} %negate_multiply_fusion, f32[1536,512]{1,0:T(8,128)S(1)} %copy-done.8), kind=kOutput, calls=%fused_computation.15 | convolution fusion | flops 2419851264 | bytes 7346176 | tf_op jit(solution)/shard_map/transpose(jvp())/dot_general | solution.py:19
  34.1 7.6 %fusion.18 = (f32[512]{0:T(512)S(1)}, f32[1536,512]{1,0:T(8,128)}) fusion(f32[1536,512]{1,0:T(8,128)S(1)} %copy-done.8, f32[512,512]{1,0:T(8,128)S(1)} %copy-done.1, f32[1536,512]{0,1:T(8,128)S(1)} %get-tuple-element.16, f32[1536]{0:T(1024)S(1)} %negate_multiply_fusion), kind=kOutput, calls=%fused_computation.36 | convolution fusion | flops 2424569344 | bytes 10493952 | tf_op jit(solution)/shard_map/transpose(jvp())/dot_general | solution.py:19
  41.8 0.6 concatenate.3.refs_3_
  42.4 101.6 %adasum_totals.1 = (f32[1536,512]{1,0:T(8,128)}, f32[512,512]{1,0:T(8,128)}, f32[8,512]{1,0:T(8,128)}) custom-call(f32[1536,1536]{1,0:T(8,128)} %refs_0_.1, f32[1536,512]{1,0:T(8,128)} %get-tuple-element.24.refs_1_, f32[512,512]{1,0:T(8,128)} %fusion.3.refs_2_, f32[8,512]{1,0:T(8,128)} %concatenate.3.refs_3_), custom_call_target="tpu_custom_call" | custom-call | tf_op jit(solution)/shard_map/adasum_totals/pallas_call | solution.py:464
  144.0 4.4 %multiply_subtract_fusion = f32[1536,512]{1,0:T(8,128)} fusion(f32[1536,512]{1,0:T(8,128)S(1)} %copy-done, f32[1536,512]{1,0:T(8,128)} %get-tuple-element.9), kind=kLoop, calls=%fused_computation.6 | loop fusion | flops 1572864 | bytes 9437184 | tf_op jit(solution)/shard_map/sub | solution.py:502
  148.5 0.6 sub.41
  149.0 0.6 sub.40
  149.6 0.6 sub.39
  150.2 0.6 sub.37
  150.8 1.2 multiply_subtract_fusion.1
  (18 shorter events, 0.1 us)
Async XLA Ops:
  13.5 2.4 %copy-start.6 = (f32[512]{0:T(512)S(1)}, f32[512]{0:T(512)}, u32[]{:S(2)}) copy-start(f32[512]{0:T(512)} %param.13) | copy-start | bytes 6148
  21.1 0.7 copy-start.3
  21.1 0.7 copy-start.4
  26.1 1.9 %copy-start.8 = (f32[1536,512]{1,0:T(8,128)S(1)}, f32[1536,512]{1,0:T(8,128)}, u32[]{:S(2)}) copy-start(f32[1536,512]{1,0:T(8,128)} %convolution_add_fusion.1) | copy-start | bytes 9437188
  28.0 6.2 %copy-start.1 = (f32[512,512]{1,0:T(8,128)S(1)}, f32[512,512]{1,0:T(8,128)}, u32[]{:S(2)}) copy-start(f32[512,512]{1,0:T(8,128)} %param.12) | copy-start | bytes 3145732
  42.4 101.6 %copy-start = (f32[1536,512]{1,0:T(8,128)S(1)}, f32[1536,512]{1,0:T(8,128)}, u32[]{:S(2)}) copy-start(f32[1536,512]{1,0:T(8,128)} %param.10) | copy-start | bytes 9437188
  144.0 4.4 %copy-start.5 = (f32[8,512]{1,0:T(8,128)S(1)}, f32[8,512]{1,0:T(8,128)}, u32[]{:S(2)}) copy-start(f32[8,512]{1,0:T(8,128)} %get-tuple-element.10) | copy-start | bytes 49156
  144.0 6.2 %copy-start.7 = (f32[512]{0:T(512)S(1)}, f32[512]{0:T(512)}, u32[]{:S(2)}) copy-start(f32[512]{0:T(512)} %param.11) | copy-start | bytes 6148
  144.0 6.8 %copy-start.2 = (f32[512,512]{1,0:T(8,128)S(1)}, f32[512,512]{1,0:T(8,128)}, u32[]{:S(2)}) copy-start(f32[512,512]{1,0:T(8,128)} %get-tuple-element.11) | copy-start | bytes 3145732

commit v4 on v3

--- a/solution.py
+++ b/solution.py
@@ -418,7 +418,7 @@
     first = tensor(1, g_first, out_first, per_first)
     next(second)
     give(1, far[cut:])
-    for _ in range(5):
+    for _ in range(8):
         next(second)
     arrived(vec_out)
     vec_total = vec_avg[0]
@@ -481,7 +481,7 @@
             pltpu.SemaphoreType.DMA((2,)),
         ],
         compiler_params=pltpu.CompilerParams(
-            collective_id=0, has_side_effects=True, vmem_limit_bytes=56 * 2**20
+            collective_id=0, has_side_effects=True, vmem_limit_bytes=40 * 2**20
         ),
         name="adasum_totals",
     )(edges, delta, second, vectors)

time: 154 us -> 148 us (0.961)
  Pallas kernels: 102 us -> 98.3 us
  other arithmetic: 13.6 us -> 11.6 us
    pallas_call x1, Pallas kernels: 102 us -> 98.3 us  [adasum_totals(): pl.pallas_call(functools.partial(comm_kernel, sz), out_shape=[jax.ShapeDt...]
    sub x6, other arithmetic: 7.92 us -> 5.96 us  [new(): return param - step_rate * (total / avg_count)]
where the time goes in v4:
time: 148 us; the launch traced here: 146 us
  Pallas kernels  98.3 us (66%)
  matrix products  29.8 us (20%)
  other arithmetic  11.6 us (8%)
  local copies, waits for them, and re-layouts  5.49 us (4%)
    pallas_call x1, Pallas kernels, adasum_totals(): pl.pallas_call(functools.partial(comm_kernel, sz), out_shape=[jax.ShapeDt...  98.3 us
    dot_general x3, matrix products, local_loss(): jnp.dot(hidden, w_second, precision=prec, preferred_element_type=jnp.floa...  17.6 us
    dot_general x1, matrix products, local(): jnp.dot(edges, w_first, precision=prec, preferred_element_type=jnp.float32)  12.2 us
    sub x6, other arithmetic, new(): return param - step_rate * (total / avg_count)  5.96 us
    unnamed x19, local copies, waits for them, and re-layouts  5.46 us

profile of v4, /device:TPU:0, one launch (start us, length us, event | category | flops | bytes accessed | tf_op | source)
XLA Modules:
  0.0 146.0 jit_solution(14247041478352707254)
XLA Ops:
  0.6 0.7 broadcast_multiply_fusion.1
  1.3 12.2 %convolution_add_fusion.1 = f32[1536,512]{1,0:T(8,128)} fusion(f32[1536,1536]{1,0:T(8,128)} %refs_0_.1, f32[1536,512]{1,0:T(8,128)} %param.10, f32[512]{0:T(512)} %param.11), kind=kOutput, calls=%fused_computation.3 | convolution fusion | flops 7248543744 | bytes 15730688 | tf_op jit(solution)/shard_map/dot_general | solution.py:492
  13.5 2.4 %copy.14 = f32[1536,512]{0,1:T(8,128)S(1)} copy(f32[1536,512]{1,0:T(8,128)} %param.9) | data formatting | bytes 6291456 | tf_op args[1]
  15.9 5.2 %fusion.17 = (f32[1536]{0:T(1024)S(1)}, f32[1536,512]{0,1:T(8,128)S(1)}) fusion(f32[512]{0:T(512)S(1)} %copy-done.6, f32[512,512]{1,0:T(8,128)} %param.12, f32[1536,512]{1,0:T(8,128)} %convolution_add_fusion.1), kind=kOutput, calls=%fused_computation.35 | convolution fusion | flops 2420636160 | bytes 7348224 | tf_op jit(solution)/shard_map/jvp()/dot_general | solution.py:19
  21.1 0.0 copy-start.5
  21.2 0.4 multiply_reduce_fusion.2
  21.6 0.2 copy-done.4
  21.8 0.0 copy-done.5
  21.8 2.7 %multiply_reduce_fusion.3 = (f32[512]{0:T(512)S(1)}, f32[512]{0:T(512)S(1)}, f32[1536]{0:T(1024)S(1)}) fusion(f32[1536,512]{0,1:T(8,128)S(1)} %copy.14, f32[512]{0:T(512)S(1)} %copy-done.5, f32[512]{0:T(512)S(1)} %copy-done.4, f32[1536]{0:T(1024)S(1)} %fusion.13, f32[1536,512]{0,1:T(8,128)S(1)} %get-tuple-element.22, f32[1536]{0:T(1024)S(1)} %broadcast_multiply_fusion, ...), kind=kLoop, calls=%fused_computation.13 | loop fusion | flops 9434624 | bytes 6320128 | tf_op jit(solution)/shard_map/transpose(jvp())/reduce_sum | solution.py:23
  24.5 1.5 %fusion.16 = (f32[1536]{0:T(1024)S(1)}, f32[1536,512]{0,1:T(8,128)S(1)}) fusion(f32[1536]{0:T(1024)S(1)} %multiply_multiply_fusion, f32[512]{0:T(512)S(1)} %broadcast_multiply_fusion.1, f32[1536,512]{0,1:T(8,128)S(1)} %copy.14, f32[512]{0:T(512)S(1)} %copy-done.5, f32[512]{0:T(512)S(1)} %copy-done.4, f32[1536]{0:T(1024)S(1)} %fusion.13, ...), kind=kLoop, calls=%fused_computation.34 | loop fusion | flops 8649216 | bytes 9467904 | tf_op jit(solution)/shard_map/transpose(jvp())/reduce_sum | solution.py:21
  26.1 0.3 add_reduce_fusion
  26.4 1.6 %copy-done.8 = f32[1536,512]{1,0:T(8,128)S(1)} copy-done((f32[1536,512]{1,0:T(8,128)S(1)}, f32[1536,512]{1,0:T(8,128)}, u32[]{:S(2)}) %copy-start.8) | copy-done | bytes 3145752
  27.9 6.2 %fusion.3.refs_2_ = f32[512,512]{1,0:T(8,128)} fusion(f32[1536,512]{0,1:T(8,128)S(1)} %get-tuple-element.16, f32[1536]{0:T(1024)S(1)} %negate_multiply_fusion, f32[1536,512]{1,0:T(8,128)S(1)} %copy-done.8), kind=kOutput, calls=%fused_computation.15 | convolution fusion | flops 2419851264 | bytes 7346176 | tf_op jit(solution)/shard_map/transpose(jvp())/dot_general | solution.py:19
  34.1 6.2 %fusion.18 = (f32[512]{0:T(512)S(1)}, f32[1536,512]{1,0:T(8,128)S(1)}) fusion(f32[1536,512]{1,0:T(8,128)S(1)} %copy-done.8, f32[512,512]{1,0:T(8,128)S(1)} %copy-done.2, f32[1536,512]{0,1:T(8,128)S(1)} %get-tuple-element.16, f32[1536]{0:T(1024)S(1)} %negate_multiply_fusion), kind=kOutput, calls=%fused_computation.36 | convolution fusion | flops 2424569344 | bytes 10493952 | tf_op jit(solution)/shard_map/transpose(jvp())/dot_general | solution.py:19
  40.4 0.0 copy-start
  40.4 1.2 copy-done
  41.6 98.3 %adasum_totals.1 = (f32[1536,512]{1,0:T(8,128)S(1)}, f32[512,512]{1,0:T(8,128)S(1)}, f32[8,512]{1,0:T(8,128)S(1)}) custom-call(f32[1536,1536]{1,0:T(8,128)} %refs_0_.1, f32[1536,512]{1,0:T(8,128)S(1)} %get-tuple-element.24.refs_1_, f32[512,512]{1,0:T(8,128)S(1)} %copy-done, f32[8,512]{1,0:T(8,128)S(1)} %concatenate.3.refs_3_), custom_call_target="tpu_custom_call" | custom-call | tf_op jit(solution)/shard_map/adasum_totals/pallas_call | solution.py:464
  140.0 0.0 copy-start.7
  140.0 2.5 %multiply_subtract_fusion = f32[1536,512]{1,0:T(8,128)} fusion(f32[1536,512]{1,0:T(8,128)S(1)} %copy-done.1, f32[1536,512]{1,0:T(8,128)S(1)} %get-tuple-element.9), kind=kLoop, calls=%fused_computation.6 | loop fusion | flops 1572864 | bytes 9437184 | tf_op jit(solution)/shard_map/sub | solution.py:502
  142.4 0.6 sub.41
  143.0 0.6 sub.40
  143.6 0.6 sub.39
  144.2 0.6 sub.37
  144.8 1.2 multiply_subtract_fusion.1
  (18 shorter events, 0.1 us)
Async XLA Ops:
  13.5 2.4 %copy-start.6 = (f32[512]{0:T(512)S(1)}, f32[512]{0:T(512)}, u32[]{:S(2)}) copy-start(f32[512]{0:T(512)} %param.13) | copy-start | bytes 6148
  21.1 0.7 copy-start.4
  21.1 0.7 copy-start.5
  26.0 1.9 %copy-start.8 = (f32[1536,512]{1,0:T(8,128)S(1)}, f32[1536,512]{1,0:T(8,128)}, u32[]{:S(2)}) copy-start(f32[1536,512]{1,0:T(8,128)} %convolution_add_fusion.1) | copy-start | bytes 9437188
  27.9 6.2 %copy-start.2 = (f32[512,512]{1,0:T(8,128)S(1)}, f32[512,512]{1,0:T(8,128)}, u32[]{:S(2)}) copy-start(f32[512,512]{1,0:T(8,128)} %param.12) | copy-start | bytes 3145732
  40.4 1.2 copy-start
  41.6 98.3 %copy-start.1 = (f32[1536,512]{1,0:T(8,128)S(1)}, f32[1536,512]{1,0:T(8,128)}, u32[]{:S(2)}) copy-start(f32[1536,512]{1,0:T(8,128)} %param.10) | copy-start | bytes 9437188
  140.0 4.2 %copy-start.7 = (f32[512]{0:T(512)S(1)}, f32[512]{0:T(512)}, u32[]{:S(2)}) copy-start(f32[512]{0:T(512)} %param.11) | copy-start | bytes 6148
  140.0 4.8 %copy-start.3 = (f32[512,512]{1,0:T(8,128)S(1)}, f32[512,512]{1,0:T(8,128)}, u32[]{:S(2)}) copy-start(f32[512,512]{1,0:T(8,128)} %param.12) | copy-start | bytes 3145732
